TPU v7x, 128 devices: a whole 4x4x4 slice. The times are simulated.
128 devices in a mesh: row: 8 (over x, core), col: 16 (over y, z).
Axes of the slice: x: 4, y: 4, z: 4, core: 2. Of those that a mesh axis runs over, the one named last changes fastest.
Arguments:
- left_factor: bfloat16 [4, 2048, 24, 4096], P(None, 'row', None, 'col'), may hold values from -0.01953125 to 0.01953125
- prev_solution: bfloat16 [24, 4096, 512], P('row', 'col'), may hold values from -6 to 6
- cross: bfloat16 [4, 2048, 512], P(None, 'row'), may hold values from -6 to 6
- inverses: bfloat16 [2, 2, 2048, 1, 4096], P(None, None, 'row', None, 'col'), as said below
- coupling: bfloat16 [2, 2048, 1, 4096], P(None, 'row', None, 'col'), may hold values from -0.09375 to 0.09375
- prior_cov: float32 [512, 512], P('col'), may hold values from -6 to 6
Outputs:
- solved: bfloat16 [4, 2048, 512], P(None, 'row')
- pred_cov: float32 [512, 512], P('col')
Inputs may be any that keep to these rules, and one draw needn't show every extreme that they name: Each block of inverses is lower triangular in natural order, with diagonal entries from 0.5 to 1.5.
All inputs are finite; a program needn't handle non-finite values.
Results may differ from a plain program's by a relative error of at most 0.0056.
Values may be sent and summed in bfloat16 or wider, within the bound.
No kernel may reach another device: no remote copies, remote signals or barrier semaphores. Data moves between devices by JAX's collectives and lax.ppermute only.
A program may use at most 64 MiB of HBM per device.

v0:
```python
import jax
import jax.numpy as jnp
from jax import lax
from jax.sharding import PartitionSpec as P

S = 8192


def from_root(shard, axis, root):
    return lax.dynamic_index_in_dim(lax.all_gather(shard, axis), root, 0, keepdims=False)


def filled_up(lines, peers):
    spare = -len(lines) % peers
    return jnp.pad(lines, [(0, spare)] + [(0, 0)] * (lines.ndim - 1))


def in_order(blocks, dim):
    shape = list(blocks.shape[1:])
    shape[dim] *= blocks.shape[0]
    return jnp.moveaxis(blocks, 0, dim).reshape(shape)


def from_everyone(shard, axis):
    peers = lax.axis_size(axis)
    return lax.all_to_all(
        jnp.broadcast_to(shard[None], (peers, *shard.shape)), axis, 0, 0, tiled=True
    )


def gather_directly(shard, axis, dim):
    return in_order(from_everyone(shard, axis), dim)


def cut_along(shard, dim, peers):
    shape = shard.shape
    blocks = shard.reshape(*shape[:dim], peers, shape[dim] // peers, *shape[dim + 1 :])
    return jnp.moveaxis(blocks, dim, 0)


def sent_and_summed(shard, axis, dim):
    blocks = cut_along(shard, dim, lax.axis_size(axis))
    arrived = lax.all_to_all(blocks, axis, split_axis=0, concat_axis=0, tiled=True)
    return arrived.sum(axis=0)


def sum_by_parts(shard, axes):
    lines = shard.reshape(-1, shard.shape[-1])
    padded = filled_up(lines, lax.axis_size(axes))
    whole = gather_directly(sent_and_summed(padded, axes, 0), axes, 0)
    return lax.slice_in_dim(whole, 0, len(lines)).reshape(shard.shape)


def over_copies(shard, axis):
    return from_everyone(shard, axis).astype(jnp.float32).sum(axis=0)


def apply_block(matrix, values):
    return jnp.einsum("atbu,bum->atm", matrix, values, preferred_element_type=jnp.float32)


def spread_rows(values):
    n_row = lax.axis_size("row")
    n_col = lax.axis_size("col")
    col_id = lax.axis_index("col")
    rounds, tile, sites = values.shape
    group = n_col // n_row
    grouped = values.reshape(rounds // group, group, tile, sites)
    picked = lax.dynamic_index_in_dim(grouped, col_id // n_row, 1, keepdims=False)
    return from_root(picked, "row", col_id % n_row)


def column_sum(values):
    return sum_by_parts(values, "col")


def solve_rounded(values):
    return sum_by_parts(values, "col").astype(jnp.bfloat16)


def outer_rows(solution):
    share = solution.shape[2] // lax.axis_size("col")
    own = lax.dynamic_slice_in_dim(solution, lax.axis_index("col") * share, share, 2)
    return jnp.einsum("atm,atn->mn", own, solution, preferred_element_type=jnp.float32)


def body(left_factor, prev_solution, cross, inverses, coupling, prior_cov):
    half = coupling.shape[0]
    pre = jnp.einsum(
        "atbu,bum->atm",
        left_factor,
        lax.all_gather(prev_solution, "row", axis=0, tiled=True),
        preferred_element_type=jnp.float32,
    )
    cross_first = cross[:half].astype(jnp.float32)
    cross_second = cross[half:].astype(jnp.float32)
    pre_first = sum_by_parts(pre[:half], "col")
    first_rhs = (cross_first - pre_first).astype(jnp.bfloat16)
    solved_first = solve_rounded(apply_block(inverses[0], spread_rows(first_rhs)))
    linked = column_sum(pre[half:] + apply_block(coupling, spread_rows(solved_first)))
    second_rhs = (cross_second - linked).astype(jnp.bfloat16)
    solved_second = solve_rounded(apply_block(inverses[1], spread_rows(second_rhs)))
    solved_all = jnp.concatenate([solved_first, solved_second], axis=0)
    outer_total = over_copies(outer_rows(solved_all).astype(jnp.bfloat16), "row").astype(
        jnp.float32
    )
    pred_cov = prior_cov - outer_total / S
    return (solved_all, pred_cov)


def solution(mesh):
    placed = (
        P(None, "row", None, "col"),
        P("row", "col", None),
        P(None, "row", None),
        P(None, None, "row", None, "col"),
        P(None, "row", None, "col"),
        P("col", None),
    )
    return jax.shard_map(
        body,
        mesh=mesh,
        in_specs=placed,
        out_specs=(P(None, "row", None), P("col", None)),
        check_vma=False,
    )
```

profile of v0, /device:TPU:1, one launch (start us, length us, event | category | flops | bytes accessed | tf_op | source)
XLA Modules:
  0.0 326.6 jit_solution(15073894378876235162)
XLA Ops:
  7.9 46.3 %all-gather.8.cloned.1.call-done = bf16[24,256,512]{2,1,0:T(8,128)(2,1)} async-done(((bf16[3,256,512]{2,1,0:T(8,128)(2,1)}), bf16[24,256,512]{2,1,0:T(8,128)(2,1)}) %all-gather.8.cloned.1.call-update) | async-done | bytes 6291472 | tf_op jit(solution)/shard_map/all_gather | solution.py:92
  54.2 14.2 %fusion.3 = f32[4,256,512]{2,1,0:T(8,128)S(1)} fusion(bf16[24,256,512]{2,1,0:T(8,128)(2,1)} %all-gather.8.cloned.1.call-done, bf16[4,256,24,256]{3,2,1,0:T(8,128)(2,1)} %param.6), kind=kOutput, calls=%fused_computation.3 | convolution fusion | flops 6442450944 | bytes 20971520 | tf_op jit(solution)/shard_map/atbu,bum->atm/dot_general | solution.py:89
  68.5 22.4 %all_to_all.45 = f32[16,32,512]{2,1,0:T(8,128)S(1)} all-to-all(f32[16,32,512]{2,1,0:T(8,128)S(1)} %bitcast.52), channel_id=1, replica_groups=mesh['row'=8,'col'=16] {'col'}, dimensions={0} | all-to-all | bytes 2097152 | tf_op jit(solution)/shard_map/all_to_all | solution.py:43
  91.0 1.1 broadcast_in_dim.10
  92.1 3.9 %all-to-all-start.1 = ((f32[16,32,512]{2,1,0:T(8,128)}), f32[16,32,512]{2,1,0:T(8,128)S(1)}, u32[]{:S(2)}, u32[]{:S(2)}) async-start(f32[16,32,512]{2,1,0:T(8,128)} %broadcast_in_dim.10), calls=%async_computation.1 | async-start | bytes 2097152 | tf_op jit(solution)/shard_map/all_to_all | solution.py:26
  96.1 2.3 fusion.26
  98.4 12.7 %all-to-all-done.1 = f32[16,32,512]{2,1,0:T(8,128)S(1)} async-done(((f32[16,32,512]{2,1,0:T(8,128)}), f32[16,32,512]{2,1,0:T(8,128)S(1)}, u32[]{:S(2)}, u32[]{:S(2)}) %all-to-all-start.1) | async-done | bytes 1048608 | tf_op jit(solution)/shard_map/all_to_all | solution.py:26
  111.0 1.7 fusion.11
  112.9 1.8 fusion.27
  114.6 22.8 %all-gather.10.cloned.1.call-done = bf16[8,256,512]{2,1,0:T(8,128)(2,1)} async-done(((bf16[1,256,512]{2,1,0:T(8,128)(2,1)}), bf16[8,256,512]{2,1,0:T(8,128)(2,1)}) %all-gather.10.cloned.1.call-update) | async-done | bytes 2097168 | tf_op jit(solution)/shard_map/all_gather | solution.py:10
  137.5 1.2 convolution_bitcast_fusion.2
  138.7 22.4 %all_to_all.46 = f32[16,32,512]{2,1,0:T(8,128)S(1)} all-to-all(f32[16,32,512]{2,1,0:T(8,128)S(1)} %convolution_bitcast_fusion.2), channel_id=1, replica_groups=mesh['row'=8,'col'=16] {'col'}, dimensions={0} | all-to-all | bytes 2097152 | tf_op jit(solution)/shard_map/all_to_all | solution.py:43
  161.3 12.8 %all_to_all.47 = bf16[16,32,512]{2,1,0:T(8,128)(2,1)S(1)} all-to-all(bf16[16,32,512]{2,1,0:T(8,128)(2,1)S(1)} %broadcast_in_dim.11), channel_id=1, replica_groups=mesh['row'=8,'col'=16] {'col'}, dimensions={0} | all-to-all | bytes 1048576 | tf_op jit(solution)/shard_map/all_to_all | solution.py:26
  174.8 25.1 %all-gather.12.cloned.1.call-done = bf16[8,256,512]{2,1,0:T(8,128)(2,1)} async-done(((bf16[1,256,512]{2,1,0:T(8,128)(2,1)}), bf16[8,256,512]{2,1,0:T(8,128)(2,1)}) %all-gather.12.cloned.1.call-update) | async-done | bytes 2097168 | tf_op jit(solution)/shard_map/all_gather | solution.py:10
  199.9 1.2 fusion.8
  201.2 22.4 %all_to_all.48 = f32[16,32,512]{2,1,0:T(8,128)S(1)} all-to-all(f32[16,32,512]{2,1,0:T(8,128)S(1)} %bitcast.51), channel_id=1, replica_groups=mesh['row'=8,'col'=16] {'col'}, dimensions={0} | all-to-all | bytes 2097152 | tf_op jit(solution)/shard_map/all_to_all | solution.py:43
  223.8 18.5 %all_to_all.49 = f32[16,32,512]{2,1,0:T(8,128)S(1)} all-to-all(f32[16,32,512]{2,1,0:T(8,128)S(1)} %broadcast_in_dim.12), channel_id=1, replica_groups=mesh['row'=8,'col'=16] {'col'}, dimensions={0} | all-to-all | bytes 2097152 | tf_op jit(solution)/shard_map/all_to_all | solution.py:26
  243.1 25.2 %all-gather.14.cloned.1.call-done = bf16[8,256,512]{2,1,0:T(8,128)(2,1)} async-done(((bf16[1,256,512]{2,1,0:T(8,128)(2,1)}), bf16[8,256,512]{2,1,0:T(8,128)(2,1)}) %all-gather.14.cloned.1.call-update) | async-done | bytes 2097168 | tf_op jit(solution)/shard_map/all_gather | solution.py:10
  268.3 1.2 convolution_bitcast_fusion
  269.6 22.4 %all_to_all.50 = f32[16,32,512]{2,1,0:T(8,128)S(1)} all-to-all(f32[16,32,512]{2,1,0:T(8,128)S(1)} %convolution_bitcast_fusion), channel_id=1, replica_groups=mesh['row'=8,'col'=16] {'col'}, dimensions={0} | all-to-all | bytes 2097152 | tf_op jit(solution)/shard_map/all_to_all | solution.py:43
  292.1 0.8 broadcast_in_dim.13
  292.9 3.9 %all-to-all-start.7 = ((bf16[16,32,512]{2,1,0:T(8,128)(2,1)}), bf16[16,32,512]{2,1,0:T(8,128)(2,1)S(1)}, u32[]{:S(2)}, u32[]{:S(2)}) async-start(bf16[16,32,512]{2,1,0:T(8,128)(2,1)} %broadcast_in_dim.13), calls=%async_computation.7 | async-start | bytes 1048576 | tf_op jit(solution)/shard_map/all_to_all | solution.py:26
  296.8 9.1 %all-to-all-done.7 = bf16[16,32,512]{2,1,0:T(8,128)(2,1)S(1)} async-done(((bf16[16,32,512]{2,1,0:T(8,128)(2,1)}), bf16[16,32,512]{2,1,0:T(8,128)(2,1)S(1)}, u32[]{:S(2)}, u32[]{:S(2)}) %all-to-all-start.7) | async-done | bytes 524320 | tf_op jit(solution)/shard_map/all_to_all | solution.py:26
  306.6 12.9 %all_to_all.51 = bf16[8,32,512]{2,1,0:T(8,128)(2,1)S(1)} all-to-all(bf16[8,32,512]{2,1,0:T(8,128)(2,1)S(1)} %broadcast_in_dim.14), channel_id=1, replica_groups=mesh['row'=8,'col'=16] {'row'}, dimensions={0} | all-to-all | bytes 524288 | tf_op jit(solution)/shard_map/all_to_all | solution.py:26
  (32 shorter events, 4.2 us)
Async XLA Ops:
  7.2 192.8 %copy-start = (bf16[2,256,1,256]{3,1,2,0:T(8,128)(2,1)S(1)}, bf16[2,256,1,256]{3,1,2,0:T(8,128)(2,1)}, u32[]{:S(2)}) copy-start(bf16[2,256,1,256]{3,1,2,0:T(8,128)(2,1)} %param.10) | copy-start | bytes 786436
  7.2 47.1 %all-gather.8.cloned.1.call-start = ((), (), s32[]{:S(2)}) async-start(), calls=%async_computation.9 | async-start | bytes 7077888 | tf_op jit(solution)/shard_map/all_gather | solution.py:92
  92.1 19.0 %all-to-all-start.1 = ((f32[16,32,512]{2,1,0:T(8,128)}), f32[16,32,512]{2,1,0:T(8,128)S(1)}, u32[]{:S(2)}, u32[]{:S(2)}) async-start(f32[16,32,512]{2,1,0:T(8,128)} %broadcast_in_dim.10), calls=%async_computation.1 | async-start | bytes 2097152 | tf_op jit(solution)/shard_map/all_to_all | solution.py:26
  96.0 41.4 %all-gather.10.cloned.1.call-start = ((), (), s32[]{:S(2)}) async-start(), calls=%async_computation.10 | async-start | bytes 2359296 | tf_op jit(solution)/shard_map/all_gather | solution.py:10
  112.8 87.1 %all-gather.12.cloned.1.call-start = ((), (), s32[]{:S(2)}) async-start(), calls=%async_computation.11 | async-start | bytes 2359296 | tf_op jit(solution)/shard_map/all_gather | solution.py:10
  174.8 93.5 %all-gather.14.cloned.1.call-start = ((), (), s32[]{:S(2)}) async-start(), calls=%async_computation.12 | async-start | bytes 2359296 | tf_op jit(solution)/shard_map/all_gather | solution.py:10
  223.6 18.7 %copy-start.2 = (bf16[2,256,512]{2,1,0:T(8,128)(2,1)S(1)}, bf16[2,256,512]{2,1,0:T(8,128)(2,1)}, u32[]{:S(2)}) copy-start(bf16[2,256,512]{2,1,0:T(8,128)(2,1)} %get-tuple-element.2) | copy-start | bytes 1572868
  223.7 44.6 %copy-start.3 = (bf16[1,2,256,1,256]{4,2,3,1,0:T(8,128)(2,1)S(1)}, bf16[1,2,256,1,256]{4,2,3,1,0:T(8,128)(2,1)}, u32[]{:S(2)}) copy-start(bf16[1,2,256,1,256]{4,2,3,1,0:T(8,128)(2,1)} %get-tuple-element.5) | copy-start | bytes 786436
  292.9 13.1 %all-to-all-start.7 = ((bf16[16,32,512]{2,1,0:T(8,128)(2,1)}), bf16[16,32,512]{2,1,0:T(8,128)(2,1)S(1)}, u32[]{:S(2)}, u32[]{:S(2)}) async-start(bf16[16,32,512]{2,1,0:T(8,128)(2,1)} %broadcast_in_dim.13), calls=%async_computation.7 | async-start | bytes 1048576 | tf_op jit(solution)/shard_map/all_to_all | solution.py:26
  306.1 14.0 %copy-start.1 = (bf16[4,256,512]{2,1,0:T(8,128)(2,1)}, bf16[4,256,512]{2,1,0:T(8,128)(2,1)S(1)}, u32[]{:S(2)}) copy-start(bf16[4,256,512]{2,1,0:T(8,128)(2,1)S(1)} %pad_maximum_fusion) | copy-start | bytes 3145732
  306.1 13.4 %copy-start.4 = (f32[32,512]{1,0:T(8,128)S(1)}, f32[32,512]{1,0:T(8,128)}, u32[]{:S(2)}) copy-start(f32[32,512]{1,0:T(8,128)} %param.11) | copy-start | bytes 196612
Sparse Core Ops, SparseCore 0:
  9.7 44.4 all-gather.7
  112.9 24.4 all-gather.9
  174.9 25.0 all-gather.11
  243.2 25.0 all-gather.13
where the time goes:
time: 327 us
  waiting for transfers between devices  142 us (43%)
  blocking collectives  134 us (41%)
  matrix products  18.3 us (6%)
  between operations  13.9 us (4%)
  starting transfers between devices  8 us (2%)
  local copies, waits for them, and re-layouts  7.02 us (2%)
  other arithmetic  3.55 us (1%)
    all_to_all x4, blocking collectives, sent_and_summed(): lax.all_to_all(blocks, axis, split_axis=0, concat_axis=0, tiled=True)  89.7 us
    all_gather x3, waiting for transfers between devices, from_root(): lax.all_gather(shard, axis)  73.1 us
    all_gather x1, waiting for transfers between devices, body(): lax.all_gather(prev_solution, 'row', axis=0, tiled=True)  46.3 us
    all_to_all x3, blocking collectives, from_everyone(): lax.all_to_all(jnp.broadcast_to(shard[None], (peers, *shard.shape)), axis...  44.1 us
    all_to_all x2, waiting for transfers between devices, from_everyone(): lax.all_to_all(jnp.broadcast_to(shard[None], (peers, *shard.shape)), axis...  21.8 us
    dot_general x1, matrix products, body(): jnp.einsum('atbu,bum->atm', left_factor, lax.all_gather(prev_solution, 'r...  14.2 us
    all_to_all x2, starting transfers between devices, from_everyone(): lax.all_to_all(jnp.broadcast_to(shard[None], (peers, *shard.shape)), axis...  7.83 us
  transfers between devices with their start and end apart: 6, of which 6 were waited for; matrix products, arithmetic and copies ran while one was open for 1% of the time, Pallas kernels for 0%

commit v1 on v0

--- a/solution.py
+++ b/solution.py
@@ -4,6 +4,22 @@
 from jax.sharding import PartitionSpec as P
 
 S = 8192
+
+
+def product_in_turn(x, axis, dim, contribution):
+    size, position, rows = (lax.axis_size(axis), lax.axis_index(axis), x.shape[dim])
+    right = [(i, (i + 1) % size) for i in range(size)]
+    left = [(i, (i - 1) % size) for i in range(size)]
+    middle = size // 2
+    from_left = from_right = x
+    total = contribution(x, position * rows)
+    for lap in range(1, middle + 1):
+        from_left = lax.ppermute(from_left, axis, right)
+        if lap < size - middle:
+            from_right = lax.ppermute(from_right, axis, left)
+            total = total + contribution(from_right, (position + lap) % size * rows)
+        total = total + contribution(from_left, (position - lap) % size * rows)
+    return total
 
 
 def from_root(shard, axis, root):
@@ -86,11 +102,16 @@
 
 def body(left_factor, prev_solution, cross, inverses, coupling, prior_cov):
     half = coupling.shape[0]
-    pre = jnp.einsum(
-        "atbu,bum->atm",
-        left_factor,
-        lax.all_gather(prev_solution, "row", axis=0, tiled=True),
-        preferred_element_type=jnp.float32,
+    pre = product_in_turn(
+        prev_solution,
+        "row",
+        0,
+        lambda own_block, offset: jnp.einsum(
+            "atbu,bum->atm",
+            lax.dynamic_slice_in_dim(left_factor, offset, own_block.shape[0], axis=2),
+            own_block,
+            preferred_element_type=jnp.float32,
+        ),
     )
     cross_first = cross[:half].astype(jnp.float32)
     cross_second = cross[half:].astype(jnp.float32)

time: 327 us -> 341 us (1.043)
  local copies, waits for them, and re-layouts: 7.02 us -> 35.6 us
  waiting for transfers between devices: 142 us -> 122 us
  starting transfers between devices: 8 us -> 16.7 us
    all_gather x1 -> x0, waiting for transfers between devices: 46.3 us -> none  [body(): lax.all_gather(prev_solution, 'row', axis=0, tiled=True)]
    dynamic_slice x0 -> x1, local copies, waits for them, and re-layouts: none -> 27.8 us  [body(): lax.dynamic_slice_in_dim(left_factor, offset, own_block.shape[0], axis=2)]
    ppermute x0 -> x7, waiting for transfers between devices: none -> 17.5 us  [the longest x4 9.69 us: product_in_turn(): from_left = lax.ppermute(from_left, axis, right)]
    all_gather x3, waiting for transfers between devices: 73.1 us -> 85.4 us  [from_root(): lax.all_gather(shard, axis)]
    ppermute x0 -> x7, starting transfers between devices: none -> 8.78 us  [the longest x4 7.99 us: product_in_turn(): from_left = lax.ppermute(from_left, axis, right)]
    dot_general x1 -> x8, matrix products: 14.2 us -> 13.8 us  [body(): jnp.einsum('atbu,bum->atm', lax.dynamic_slice_in_dim(left_factor, offset,...]
  transfers between devices with their start and end apart: 6 -> 12, of which waited for: 6 -> 9; matrix products, arithmetic and copies ran while one was open for 1% -> 13% of each run, Pallas kernels for 0% -> 0%
where the time goes in v1:
time: 341 us; the launch traced here: 340 us
  blocking collectives  131 us (38%)
  waiting for transfers between devices  122 us (36%)
  local copies, waits for them, and re-layouts  35.6 us (10%)
  matrix products  18 us (5%)
  starting transfers between devices  16.7 us (5%)
  between operations  14 us (4%)
  other arithmetic  3.57 us (1%)
    all_to_all x4, blocking collectives, sent_and_summed(): lax.all_to_all(blocks, axis, split_axis=0, concat_axis=0, tiled=True)  86.6 us
    all_gather x3, waiting for transfers between devices, from_root(): lax.all_gather(shard, axis)  85.4 us
    all_to_all x3, blocking collectives, from_everyone(): lax.all_to_all(jnp.broadcast_to(shard[None], (peers, *shard.shape)), axis...  44 us
    dynamic_slice x1, local copies, waits for them, and re-layouts, body(): lax.dynamic_slice_in_dim(left_factor, offset, own_block.shape[0], axis=2)  27.8 us
    all_to_all x2, waiting for transfers between devices, from_everyone(): lax.all_to_all(jnp.broadcast_to(shard[None], (peers, *shard.shape)), axis...  18.7 us
    dot_general x8, matrix products, body(): jnp.einsum('atbu,bum->atm', lax.dynamic_slice_in_dim(left_factor, offset,...  13.8 us
    ppermute x4, waiting for transfers between devices, product_in_turn(): from_left = lax.ppermute(from_left, axis, right)  9.69 us
    ppermute x4, starting transfers between devices, product_in_turn(): from_left = lax.ppermute(from_left, axis, right)  7.99 us
  transfers between devices with their start and end apart: 12, of which 9 were waited for; matrix products, arithmetic and copies ran while one was open for 13% of the time, Pallas kernels for 0%

profile of v1, /device:TPU:1, one launch (start us, length us, event | category | flops | bytes accessed | tf_op | source)
XLA Modules:
  0.0 340.0 jit_solution(17009649911504501715)
XLA Ops:
  7.2 2.6 collective-permute-start.1
  9.8 9.2 %collective-permute-done.1 = bf16[3,256,512]{2,1,0:T(8,128)(2,1)} collective-permute-done((bf16[3,256,512]{2,1,0:T(8,128)(2,1)}, bf16[3,256,512]{2,1,0:T(8,128)(2,1)}, u32[]{:S(2)}, u32[]{:S(2)}) %collective-permute-start.1) | collective-permute-done | bytes 786464 | tf_op jit(solution)/shard_map/ppermute | solution.py:17
  19.0 2.5 collective-permute-start.3
  21.5 27.8 %constant_dynamic-slice_fusion.1 = (bf16[4,256,3,256]{3,2,1,0:T(4,128)(2,1)}, bf16[4,256,3,256]{3,2,1,0:T(4,128)(2,1)}, bf16[4,256,3,256]{3,2,1,0:T(4,128)(2,1)S...) fusion(bf16[4,256,24,256]{3,2,1,0:T(8,128)(2,1)} %param.6, ...), kind=kLoop, calls=%fused_computation.58 | loop fusion | bytes 25165856 | tf_op jit(solution)/shard_map/dynamic_slice | solution.py:111
  49.4 2.7 fusion.13
  53.8 2.3 fusion.11
  56.1 2.3 fusion.9
  58.4 2.9 collective-permute-done.2
  62.0 2.3 fusion.5
  68.0 4.9 %collective-permute-done.4 = bf16[3,256,512]{2,1,0:T(8,128)(2,1)S(1)} collective-permute-done((bf16[3,256,512]{2,1,0:T(8,128)(2,1)S(1)}, bf16[3,256,512]{2,1,0:T(8,128)(2,1)S(1)}, u32[]{:S(2)}, u32[]{:S(2)}) %collective-permute-start.4) | collective-permute-done | bytes 786464 | tf_op jit(solution)/shard_map/ppermute | solution.py:19
  76.1 19.3 %all_to_all.45 = f32[16,32,512]{2,1,0:T(8,128)S(1)} all-to-all(f32[16,32,512]{2,1,0:T(8,128)S(1)} %bitcast.106), channel_id=1, replica_groups=mesh['row'=8,'col'=16] {'col'}, dimensions={0} | all-to-all | bytes 2097152 | tf_op jit(solution)/shard_map/all_to_all | solution.py:59
  96.6 3.7 %all-to-all-start.1 = ((f32[16,32,512]{2,1,0:T(8,128)}), f32[16,32,512]{2,1,0:T(8,128)S(1)}, u32[]{:S(2)}, u32[]{:S(2)}) async-start(f32[16,32,512]{2,1,0:T(8,128)} %broadcast_in_dim.10), calls=%async_computation.1 | async-start | bytes 2097152 | tf_op jit(solution)/shard_map/all_to_all | solution.py:42
  102.5 9.5 %all-to-all-done.1 = f32[16,32,512]{2,1,0:T(8,128)S(1)} async-done(((f32[16,32,512]{2,1,0:T(8,128)}), f32[16,32,512]{2,1,0:T(8,128)S(1)}, u32[]{:S(2)}, u32[]{:S(2)}) %all-to-all-start.1) | async-done | bytes 1048608 | tf_op jit(solution)/shard_map/all_to_all | solution.py:42
  115.8 35.0 %all-gather.7.cloned.1.call-done = bf16[8,256,512]{2,1,0:T(8,128)(2,1)} async-done(((bf16[1,256,512]{2,1,0:T(8,128)(2,1)}), bf16[8,256,512]{2,1,0:T(8,128)(2,1)}) %all-gather.7.cloned.1.call-update) | async-done | bytes 2097168 | tf_op jit(solution)/shard_map/all_gather | solution.py:26
  152.1 22.4 %all_to_all.46 = f32[16,32,512]{2,1,0:T(8,128)S(1)} all-to-all(f32[16,32,512]{2,1,0:T(8,128)S(1)} %convolution_bitcast_fusion.2), channel_id=1, replica_groups=mesh['row'=8,'col'=16] {'col'}, dimensions={0} | all-to-all | bytes 2097152 | tf_op jit(solution)/shard_map/all_to_all | solution.py:59
  174.7 12.7 %all_to_all.47 = bf16[16,32,512]{2,1,0:T(8,128)(2,1)S(1)} all-to-all(bf16[16,32,512]{2,1,0:T(8,128)(2,1)S(1)} %broadcast_in_dim.11), channel_id=1, replica_groups=mesh['row'=8,'col'=16] {'col'}, dimensions={0} | all-to-all | bytes 1048576 | tf_op jit(solution)/shard_map/all_to_all | solution.py:42
  188.2 25.1 %all-gather.9.cloned.1.call-done = bf16[8,256,512]{2,1,0:T(8,128)(2,1)} async-done(((bf16[1,256,512]{2,1,0:T(8,128)(2,1)}), bf16[8,256,512]{2,1,0:T(8,128)(2,1)}) %all-gather.9.cloned.1.call-update) | async-done | bytes 2097168 | tf_op jit(solution)/shard_map/all_gather | solution.py:26
  214.6 22.4 %all_to_all.48 = f32[16,32,512]{2,1,0:T(8,128)S(1)} all-to-all(f32[16,32,512]{2,1,0:T(8,128)S(1)} %bitcast.105), channel_id=1, replica_groups=mesh['row'=8,'col'=16] {'col'}, dimensions={0} | all-to-all | bytes 2097152 | tf_op jit(solution)/shard_map/all_to_all | solution.py:59
  237.2 18.5 %all_to_all.49 = f32[16,32,512]{2,1,0:T(8,128)S(1)} all-to-all(f32[16,32,512]{2,1,0:T(8,128)S(1)} %broadcast_in_dim.12), channel_id=1, replica_groups=mesh['row'=8,'col'=16] {'col'}, dimensions={0} | all-to-all | bytes 2097152 | tf_op jit(solution)/shard_map/all_to_all | solution.py:42
  256.5 25.2 %all-gather.11.cloned.1.call-done = bf16[8,256,512]{2,1,0:T(8,128)(2,1)} async-done(((bf16[1,256,512]{2,1,0:T(8,128)(2,1)}), bf16[8,256,512]{2,1,0:T(8,128)(2,1)}) %all-gather.11.cloned.1.call-update) | async-done | bytes 2097168 | tf_op jit(solution)/shard_map/all_gather | solution.py:26
  283.0 22.4 %all_to_all.50 = f32[16,32,512]{2,1,0:T(8,128)S(1)} all-to-all(f32[16,32,512]{2,1,0:T(8,128)S(1)} %convolution_bitcast_fusion), channel_id=1, replica_groups=mesh['row'=8,'col'=16] {'col'}, dimensions={0} | all-to-all | bytes 2097152 | tf_op jit(solution)/shard_map/all_to_all | solution.py:59
  306.3 3.9 %all-to-all-start.7 = ((bf16[16,32,512]{2,1,0:T(8,128)(2,1)}), bf16[16,32,512]{2,1,0:T(8,128)(2,1)S(1)}, u32[]{:S(2)}, u32[]{:S(2)}) async-start(bf16[16,32,512]{2,1,0:T(8,128)(2,1)} %broadcast_in_dim.13), calls=%async_computation.7 | async-start | bytes 1048576 | tf_op jit(solution)/shard_map/all_to_all | solution.py:42
  310.2 9.2 %all-to-all-done.7 = bf16[16,32,512]{2,1,0:T(8,128)(2,1)S(1)} async-done(((bf16[16,32,512]{2,1,0:T(8,128)(2,1)}), bf16[16,32,512]{2,1,0:T(8,128)(2,1)S(1)}, u32[]{:S(2)}, u32[]{:S(2)}) %all-to-all-start.7) | async-done | bytes 524320 | tf_op jit(solution)/shard_map/all_to_all | solution.py:42
  320.0 12.8 %all_to_all.51 = bf16[8,32,512]{2,1,0:T(8,128)(2,1)S(1)} all-to-all(bf16[8,32,512]{2,1,0:T(8,128)(2,1)S(1)} %broadcast_in_dim.14), channel_id=1, replica_groups=mesh['row'=8,'col'=16] {'row'}, dimensions={0} | all-to-all | bytes 524288 | tf_op jit(solution)/shard_map/all_to_all | solution.py:42
  (65 shorter events, 24.3 us)
Async XLA Ops:
  7.2 206.2 %copy-start = (bf16[2,256,1,256]{3,1,2,0:T(8,128)(2,1)S(1)}, bf16[2,256,1,256]{3,1,2,0:T(8,128)(2,1)}, u32[]{:S(2)}) copy-start(bf16[2,256,1,256]{3,1,2,0:T(8,128)(2,1)} %param.10) | copy-start | bytes 786436
  7.2 11.9 %collective-permute-start.1 = (bf16[3,256,512]{2,1,0:T(8,128)(2,1)}, bf16[3,256,512]{2,1,0:T(8,128)(2,1)}, u32[]{:S(2)}, u32[]{:S(2)}) collective-permute-start(bf16[3,256,512]{2,1,0:T(8,128)(2,1)} %param.7), channel_id=1, source_target_pairs={{0,16},{16,32},{32,48},{48,64},{64,80},{80,96},{96,112},{112,0},{1... | collective-permute-start | bytes 2359304 | tf_op jit(solution)/shard_map/ppermute | solution.py:17
  9.8 39.5 %collective-permute-start = (bf16[3,256,512]{2,1,0:T(8,128)(2,1)}, bf16[3,256,512]{2,1,0:T(8,128)(2,1)}, u32[]{:S(2)}, u32[]{:S(2)}) collective-permute-start(bf16[3,256,512]{2,1,0:T(8,128)(2,1)} %param.7), channel_id=1, source_target_pairs={{0,112},{16,0},{32,16},{48,32},{64,48},{80,64},{96,80},{112,96},{1... | collective-permute-start | bytes 2359304 | tf_op jit(solution)/shard_map/ppermute | solution.py:19
  9.8 39.6 %copy-start.11 = (bf16[3,256,512]{2,1,0:T(8,128)(2,1)S(1)}, bf16[3,256,512]{2,1,0:T(8,128)(2,1)}, u32[]{:S(2)}) copy-start(bf16[3,256,512]{2,1,0:T(8,128)(2,1)} %param.7) | copy-start | bytes 2359300
  19.0 33.1 %collective-permute-start.3 = (bf16[3,256,512]{2,1,0:T(8,128)(2,1)}, bf16[3,256,512]{2,1,0:T(8,128)(2,1)}, u32[]{:S(2)}, u32[]{:S(2)}) collective-permute-start(bf16[3,256,512]{2,1,0:T(8,128)(2,1)} %collective-permute-done.1), channel_id=1, source_target_pairs={{0,16},{16,32},{32,48},{48,64},{64,80},{80,96},{96,112},{112,0},{1... | collective-permute-start | bytes 2359304 | tf_op jit(solution)/shard_map/ppermute | solution.py:17
  49.3 11.9 %collective-permute-start.2 = (bf16[3,256,512]{2,1,0:T(8,128)(2,1)}, bf16[3,256,512]{2,1,0:T(8,128)(2,1)S(1)}, u32[]{:S(2)}, u32[]{:S(2)}) collective-permute-start(bf16[3,256,512]{2,1,0:T(8,128)(2,1)} %collective-permute-done), channel_id=1, source_target_pairs={{0,112},{16,0},{32,16},{48,32},{64,48},{80,64},{96,80},{112,96},{1... | collective-permute-start | bytes 2359304 | tf_op jit(solution)/shard_map/ppermute | solution.py:19
  49.4 4.5 %copy-start.7 = (bf16[4,256,3,256]{3,2,1,0:T(4,128)(2,1)S(1)}, bf16[4,256,3,256]{3,2,1,0:T(4,128)(2,1)}, u32[]{:S(2)}) copy-start(bf16[4,256,3,256]{3,2,1,0:T(4,128)(2,1)} %get-tuple-element.8) | copy-start | bytes 4718596
  52.1 12.2 %collective-permute-start.5 = (bf16[3,256,512]{2,1,0:T(8,128)(2,1)}, bf16[3,256,512]{2,1,0:T(8,128)(2,1)S(1)}, u32[]{:S(2)}, u32[]{:S(2)}) collective-permute-start(bf16[3,256,512]{2,1,0:T(8,128)(2,1)} %collective-permute-done.3), channel_id=1, source_target_pairs={{0,16},{16,32},{32,48},{48,64},{64,80},{80,96},{96,112},{112,0},{1... | collective-permute-start | bytes 2359304 | tf_op jit(solution)/shard_map/ppermute | solution.py:17
  53.8 2.3 copy-start.6
  56.1 5.9 %copy-start.5 = (bf16[4,256,3,256]{3,2,1,0:T(4,128)(2,1)S(1)}, bf16[4,256,3,256]{3,2,1,0:T(4,128)(2,1)}, u32[]{:S(2)}) copy-start(bf16[4,256,3,256]{3,2,1,0:T(4,128)(2,1)} %get-tuple-element.5) | copy-start | bytes 4718596
  61.3 11.7 %collective-permute-start.4 = (bf16[3,256,512]{2,1,0:T(8,128)(2,1)S(1)}, bf16[3,256,512]{2,1,0:T(8,128)(2,1)S(1)}, u32[]{:S(2)}, u32[]{:S(2)}) collective-permute-start(bf16[3,256,512]{2,1,0:T(8,128)(2,1)S(1)} %collective-permute-done.2), channel_id=1, source_target_pairs={{0,112},{16,0},{32,16},{48,32},{64,48},{80,64},{96,80},{112,96},{1... | collective-permute-start | bytes 2359304 | tf_op jit(solution)/shard_map/ppermute | solution.py:19
  62.0 3.5 %copy-start.4 = (bf16[4,256,3,256]{3,2,1,0:T(4,128)(2,1)S(1)}, bf16[4,256,3,256]{3,2,1,0:T(4,128)(2,1)}, u32[]{:S(2)}) copy-start(bf16[4,256,3,256]{3,2,1,0:T(4,128)(2,1)} %get-tuple-element.6) | copy-start | bytes 4718596
  64.3 10.1 %collective-permute-start.6 = (bf16[3,256,512]{2,1,0:T(8,128)(2,1)S(1)}, bf16[3,256,512]{2,1,0:T(8,128)(2,1)S(1)}, u32[]{:S(2)}, u32[]{:S(2)}) collective-permute-start(bf16[3,256,512]{2,1,0:T(8,128)(2,1)S(1)} %collective-permute-done.5), channel_id=1, source_target_pairs={{0,16},{16,32},{32,48},{48,64},{64,80},{80,96},{96,112},{112,0},{1... | collective-permute-start | bytes 2359304 | tf_op jit(solution)/shard_map/ppermute | solution.py:17
  65.5 1.6 copy-start.3
  73.0 1.6 copy-start.1
  96.6 15.5 %all-to-all-start.1 = ((f32[16,32,512]{2,1,0:T(8,128)}), f32[16,32,512]{2,1,0:T(8,128)S(1)}, u32[]{:S(2)}, u32[]{:S(2)}) async-start(f32[16,32,512]{2,1,0:T(8,128)} %broadcast_in_dim.10), calls=%async_computation.1 | async-start | bytes 2097152 | tf_op jit(solution)/shard_map/all_to_all | solution.py:42
  100.2 50.6 %all-gather.7.cloned.1.call-start = ((), (), s32[]{:S(2)}) async-start(), calls=%async_computation.9 | async-start | bytes 2359296 | tf_op jit(solution)/shard_map/all_gather | solution.py:26
  113.8 99.5 %all-gather.9.cloned.1.call-start = ((), (), s32[]{:S(2)}) async-start(), calls=%async_computation.10 | async-start | bytes 2359296 | tf_op jit(solution)/shard_map/all_gather | solution.py:26
  188.2 93.5 %all-gather.11.cloned.1.call-start = ((), (), s32[]{:S(2)}) async-start(), calls=%async_computation.11 | async-start | bytes 2359296 | tf_op jit(solution)/shard_map/all_gather | solution.py:26
  237.0 18.7 %copy-start.8 = (bf16[2,256,512]{2,1,0:T(8,128)(2,1)S(1)}, bf16[2,256,512]{2,1,0:T(8,128)(2,1)}, u32[]{:S(2)}) copy-start(bf16[2,256,512]{2,1,0:T(8,128)(2,1)} %get-tuple-element.10) | copy-start | bytes 1572868
  237.1 44.6 %copy-start.9 = (bf16[1,2,256,1,256]{4,2,3,1,0:T(8,128)(2,1)S(1)}, bf16[1,2,256,1,256]{4,2,3,1,0:T(8,128)(2,1)}, u32[]{:S(2)}) copy-start(bf16[1,2,256,1,256]{4,2,3,1,0:T(8,128)(2,1)} %get-tuple-element.13) | copy-start | bytes 786436
  306.3 13.1 %all-to-all-start.7 = ((bf16[16,32,512]{2,1,0:T(8,128)(2,1)}), bf16[16,32,512]{2,1,0:T(8,128)(2,1)S(1)}, u32[]{:S(2)}, u32[]{:S(2)}) async-start(bf16[16,32,512]{2,1,0:T(8,128)(2,1)} %broadcast_in_dim.13), calls=%async_computation.7 | async-start | bytes 1048576 | tf_op jit(solution)/shard_map/all_to_all | solution.py:42
  319.5 14.0 %copy-start.2 = (bf16[4,256,512]{2,1,0:T(8,128)(2,1)}, bf16[4,256,512]{2,1,0:T(8,128)(2,1)S(1)}, u32[]{:S(2)}) copy-start(bf16[4,256,512]{2,1,0:T(8,128)(2,1)S(1)} %pad_maximum_fusion) | copy-start | bytes 3145732
  319.5 13.4 %copy-start.10 = (f32[32,512]{1,0:T(8,128)S(1)}, f32[32,512]{1,0:T(8,128)}, u32[]{:S(2)}) copy-start(f32[32,512]{1,0:T(8,128)} %param.11) | copy-start | bytes 196612
Sparse Core Ops, SparseCore 0:
  113.9 36.8 all-gather.6
  188.3 25.0 all-gather.8
  256.6 25.0 all-gather.10
